TPU v7x, 32 devices: a whole 2x2x4 slice. The times are simulated.
32 devices in a mesh: expert: 8 (over z, y), mp: 4 (over x, core).
Axes of the slice: x: 2, y: 2, z: 4, core: 2. Of those that a mesh axis runs over, the one named last changes fastest.
Arguments:
- queries: bfloat16 [256, 48, 128], P('expert', 'mp'), may hold values from -140 to 140
- k_cache: bfloat16 [256, 8, 128, 128], P('expert', 'mp'), may hold values from -5 to 5
- v_cache: bfloat16 [256, 8, 128, 128], P('expert', 'mp'), may hold values from -6 to 6
- lengths: int32 [256], P('expert'), may hold values from 2 to 128
- moe_input: bfloat16 [256, 6144], P('expert', 'mp'), may hold values from -40 to 40
- norm_gain: float32 [6144], P('mp'), may hold values from 0.5 to 1.5
- expert_ids: int32 [256, 2], P('expert'), may hold values from 0 to 7, all different within a row; in each aligned block of 32 rows (0 to 31, 32 to 63, ...) at most 16 rows name the same one
- combine_weights: float32 [256, 2], P('expert'), may hold values from 0.1 to 1
- capacity: int32 [8], replicated, may hold values from 8 to 16
- w_gate: bfloat16 [8, 6144, 8192], P('expert', None, 'mp'), may hold values from -0.078125 to 0.078125
- w_up: bfloat16 [8, 6144, 8192], P('expert', None, 'mp'), may hold values from -0.078125 to 0.078125
- w_down: bfloat16 [8, 8192, 6144], P('expert', 'mp'), may hold values from -0.0625 to 0.0625
Outputs:
- context: bfloat16 [256, 48, 128], P('expert', 'mp')
- layer_out: bfloat16 [256, 6144], P('expert', 'mp')
Inputs may be any that keep to these rules, and one draw needn't show every extreme that they name: `expert_ids`: within each aligned block of 32 tokens, no expert is named by more than 16 tokens; the 2 ids of a token differ.
All inputs are finite; a program needn't handle non-finite values.
Results may differ from a plain program's by a relative error of at most 0.007.
Values may be sent and summed in bfloat16 or wider, within the bound.
No kernel may reach another device: no remote copies, remote signals or barrier semaphores. Data moves between devices by JAX's collectives and lax.ppermute only.
A program may use at most 128 MiB of HBM per device.

v0:
```python
import jax
import jax.numpy as jnp
from jax import lax
from jax.sharding import PartitionSpec as P

D = 6144
EXPERTS = 8
TOP = 2


def on_device(
    queries,
    k_cache,
    v_cache,
    lengths,
    moe_input,
    norm_gain,
    expert_ids,
    combine_weights,
    capacity,
    w_gate,
    w_up,
    w_down,
):
    seq_count, head_count, head_size = queries.shape
    kv_count = k_cache.shape[1]
    group_size = head_count // kv_count
    queries_grouped = queries.reshape(seq_count, kv_count, group_size, head_size)
    scores = jnp.einsum(
        "bjgd,bjpd->bjgp", queries_grouped, k_cache, preferred_element_type=jnp.float32
    ) * head_size ** (-0.5)
    positions = jnp.arange(k_cache.shape[2])
    live_mask = positions[None, :] < lengths[:, None]
    scores = jnp.where(live_mask[:, None, None, :], scores, -jnp.inf)
    top_score = jnp.max(scores, axis=-1, keepdims=True)
    expo = jnp.exp(scores - top_score)
    probs = (expo / jnp.sum(expo, axis=-1, keepdims=True)).astype(jnp.bfloat16)
    context = jnp.einsum("bjgp,bjpd->bjgd", probs, v_cache, preferred_element_type=jnp.float32)
    context = context.astype(jnp.bfloat16).reshape(seq_count, head_count, head_size)
    tok_rows, feat_width = moe_input.shape
    experts_total = lax.axis_size("expert")
    split_count = experts_total // EXPERTS
    slot_count = tok_rows // 2
    residual = moe_input.astype(jnp.float32)
    square_sum = lax.psum(jnp.sum(residual * residual, axis=1), "mp")
    normed = (residual * lax.rsqrt(square_sum / D + 1e-05)[:, None] * norm_gain[None, :]).astype(
        jnp.bfloat16
    )
    flat_ids = expert_ids.reshape(-1)
    one_hot = (flat_ids[:, None] == jnp.arange(EXPERTS)[None, :]).astype(jnp.int32)
    earlier = jnp.cumsum(one_hot, axis=0) - one_hot
    slot_rank = jnp.sum(earlier * one_hot, axis=1)
    limits = jnp.sum(one_hot * capacity[None, :], axis=1)
    kept_mask = slot_rank < limits
    slot_id = flat_ids * slot_count + slot_rank
    select = (jnp.arange(EXPERTS * slot_count)[:, None] == slot_id[None, :]) & kept_mask[None, :]
    chosen = select.reshape(EXPERTS * slot_count, tok_rows, TOP).sum(axis=-1).astype(jnp.bfloat16)
    packed = jnp.dot(chosen, normed, preferred_element_type=jnp.float32).astype(jnp.bfloat16)
    packed_view = packed.reshape(EXPERTS, 1, slot_count, feat_width)
    outgoing = jnp.broadcast_to(
        packed_view, (EXPERTS, split_count, slot_count, feat_width)
    ).reshape(experts_total, slot_count, feat_width)
    arrived = lax.all_to_all(outgoing, "expert", split_axis=0, concat_axis=0, tiled=True)
    slot_rows = arrived.reshape(experts_total * slot_count, feat_width)
    gate_matrix = w_gate[0]
    up_matrix = w_up[0]
    piece = lax.all_gather(slot_rows, "mp", axis=1, tiled=True)
    gate_sum = jnp.dot(piece, gate_matrix, preferred_element_type=jnp.float32)
    up_sum = jnp.dot(piece, up_matrix, preferred_element_type=jnp.float32)
    hidden = (jax.nn.silu(gate_sum) * up_sum).astype(jnp.bfloat16)
    down_terms = jnp.dot(hidden, w_down[0], preferred_element_type=jnp.float32)
    result = lax.psum_scatter(
        down_terms.astype(jnp.bfloat16), "mp", scatter_dimension=1, tiled=True
    ).astype(jnp.float32)
    result = result.reshape(experts_total, slot_count, feat_width)
    returned = lax.all_to_all(
        result.astype(jnp.bfloat16), "expert", split_axis=0, concat_axis=0, tiled=True
    ).astype(result.dtype)
    gathered = returned.reshape(EXPERTS, split_count, slot_count, feat_width).sum(axis=1)
    weighted = select.astype(jnp.float32) * combine_weights.reshape(-1)[None, :]
    weighted = weighted.reshape(EXPERTS * slot_count, tok_rows, TOP).sum(axis=-1)
    added = jnp.dot(
        weighted.T,
        gathered.reshape(EXPERTS * slot_count, feat_width),
        precision=lax.Precision.HIGHEST,
        preferred_element_type=jnp.float32,
    )
    layer_out = (residual + added).astype(jnp.bfloat16)
    return (context, layer_out)


def solution(mesh):
    in_specs = (
        P("expert", "mp", None),
        P("expert", "mp", None, None),
        P("expert", "mp", None, None),
        P("expert"),
        P("expert", "mp"),
        P("mp"),
        P("expert", None),
        P("expert", None),
        P(),
        P("expert", None, "mp"),
        P("expert", None, "mp"),
        P("expert", "mp", None),
    )
    out_specs = (P("expert", "mp", None), P("expert", "mp"))
    return jax.shard_map(
        on_device, mesh=mesh, in_specs=in_specs, out_specs=out_specs, check_vma=False
    )
```

profile of v0, /device:TPU:0, one launch (start us, length us, event | category | flops | bytes accessed | tf_op | source)
XLA Modules:
  0.0 139.0 jit_solution(575278981776266259)
XLA Ops:
  7.2 0.0 copy-start
  7.2 0.0 all-gather.2.cloned.1.call-start
  7.2 0.9 copy.35
  8.1 0.1 eq.31
  8.2 0.1 fusion.36
  8.3 0.1 reduce_window_sum.11
  8.4 0.8 select_reduce_fusion.1
  9.2 0.1 reduce_sum.64
  9.4 0.1 reduce_sum.66
  9.5 0.1 copy.36
  9.6 0.1 copy.37
  9.7 0.7 multiply_add_fusion
  10.3 1.0 fusion.28
  11.4 8.4 %psum.7 = f32[32]{0:T(128)S(1)} all-reduce(f32[32]{0:T(128)S(1)} %fusion.28), channel_id=1, replica_groups=mesh['expert'=8,'mp'=4] {'mp'}, use_global_device_ids=true, to_apply=%region_8.9 | all-reduce | flops 32 | bytes 256 | tf_op jit(solution)/shard_map/psum | solution.py:45
  19.7 0.1 convert_reduce_fusion
  19.8 1.2 convolution_convert_fusion
  21.0 16.6 %all_to_all.10 = bf16[8,16,1536]{2,1,0:T(8,128)(2,1)} all-to-all(bf16[8,16,1536]{2,1,0:T(8,128)(2,1)S(1)} %bitcast.33), channel_id=1, replica_groups=mesh['expert'=8,'mp'=4] {'expert'}, dimensions={0} | all-to-all | bytes 786432 | tf_op jit(solution)/shard_map/all_to_all | solution.py:63
  37.6 0.0 all-gather.2.cloned.1.call-update
  37.7 0.0 reduce-scatter.2.cloned.1.call-start
  37.7 18.4 %all-gather.2.cloned.1.call-done = bf16[128,6144]{1,0:T(8,128)(2,1)} async-done(((bf16[128,1536]{1,0:T(8,128)(2,1)}), bf16[128,6144]{1,0:T(8,128)(2,1)}) %all-gather.2.cloned.1.call-update) | async-done | bytes 1572880 | tf_op jit(solution)/shard_map/all_gather | solution.py:67
  56.1 10.4 %fusion.5 = f32[128,2048]{1,0:T(8,128)S(1)} fusion(bf16[128,6144]{1,0:T(8,128)(2,1)} %all-gather.2.cloned.1.call-done, bf16[1,6144,2048]{2,1,0:T(8,128)(2,1)} %param.21), kind=kOutput, calls=%fused_computation.5 | convolution fusion | flops 3221225472 | bytes 27787264 | tf_op jit(solution)/shard_map/dot_general | solution.py:68
  66.6 0.0 copy-start.4
  66.6 19.4 %fusion.7 = bf16[128,6144]{1,0:T(8,128)(2,1)} fusion(bf16[1,2048,6144]{2,1,0:T(8,128)(2,1)} %param.23, bf16[128,6144]{1,0:T(8,128)(2,1)} %all-gather.2.cloned.1.call-done, bf16[1,6144,2048]{2,1,0:T(8,128)(2,1)} %param.22, f32[128,2048]{1,0:T(8,128)S(1)} %fusion.5), kind=kOutput, calls=%fused_computation.7 | convolution fusion | flops 6444810240 | bytes 54525952 | tf_op jit(solution)/shard_map/dot_general | solution.py:71
  86.0 0.0 copy-start.2
  86.0 0.0 reduce-scatter.2.cloned.1.call-update
  86.0 0.0 copy-done.4
  86.0 0.1 iota_compare_fusion.2
  86.1 28.1 %reduce-scatter.2.cloned.1.call-done = bf16[128,1536]{1,0:T(8,128)(2,1)} async-done(((bf16[128,6144]{1,0:T(8,128)(2,1)}), bf16[128,1536]{1,0:T(8,128)(2,1)}) %reduce-scatter.2.cloned.1.call-update) | async-done | bytes 393232 | tf_op jit(solution)/shard_map/reduce_scatter | solution.py:72
  114.2 5.5 %all-to-all-start.1 = ((bf16[8,16,1536]{2,1,0:T(8,128)(2,1)}), bf16[8,16,1536]{2,1,0:T(8,128)(2,1)S(1)}, u32[]{:S(2)}, u32[]{:S(2)}) async-start(bf16[8,16,1536]{2,1,0:T(8,128)(2,1)} %bitcast.34), calls=%async_computation.2 | async-start | bytes 786432 | tf_op jit(solution)/shard_map/all_to_all | solution.py:76
  119.7 0.0 copy-done
  119.7 0.0 copy-done.2
  119.7 1.2 fusion.20
  120.9 0.0 copy-start.3
  120.9 0.0 copy-start.1
  120.9 0.3 fusion.40
  121.2 2.5 %convolution_convert_fusion.1 = bf16[32,2,6,128]{3,2,1,0:T(8,128)(2,1)S(1)} fusion(bf16[32,2,128,128]{3,2,1,0:T(8,128)(2,1)} %param.14, f32[32,2,6]{2,1,0:T(2,128)S(1)} %fusion.40, f32[32,2,6,128]{3,2,1,0:T(8,128)S(1)} %fusion.20), kind=kOutput, calls=%fused_computation.17 | convolution fusion | flops 12780031 | bytes 2393600 | tf_op jit(solution)/shard_map/bjgp,bjpd->bjgd/dot_general | solution.py:38
  123.7 0.7 copy.34
  124.3 0.0 copy-done.3
  124.3 0.1 select_reduce_fusion
  124.4 6.8 %all-to-all-done.1 = bf16[8,16,1536]{2,1,0:T(8,128)(2,1)S(1)} async-done(((bf16[8,16,1536]{2,1,0:T(8,128)(2,1)}), bf16[8,16,1536]{2,1,0:T(8,128)(2,1)S(1)}, u32[]{:S(2)}, u32[]{:S(2)}) %all-to-all-start.1) | async-done | bytes 393248 | tf_op jit(solution)/shard_map/all_to_all | solution.py:76
  131.2 0.0 copy-done.1
  131.2 0.9 fusion.18
  (2 shorter events, 0.0 us)
Async XLA Ops:
  7.2 112.5 %copy-start = (bf16[32,2,128,128]{3,2,1,0:T(8,128)(2,1)S(1)}, bf16[32,2,128,128]{3,2,1,0:T(8,128)(2,1)}, u32[]{:S(2)}) copy-start(bf16[32,2,128,128]{3,2,1,0:T(8,128)(2,1)} %param.13) | copy-start | bytes 6291460
  7.2 49.0 %all-gather.2.cloned.1.call-start = ((), (), s32[]{:S(2)}) async-start(), calls=%async_computation.3 | async-start | bytes 1966080 | tf_op jit(solution)/shard_map/all_gather | solution.py:67
  37.7 76.5 %reduce-scatter.2.cloned.1.call-start = ((), (), s32[]{:S(2)}) async-start(), calls=%async_computation.4 | async-start | bytes 1966080 | tf_op jit(solution)/shard_map/reduce_scatter | solution.py:72
  66.6 19.4 %copy-start.4 = (s32[32]{0:T(128)S(1)}, s32[32]{0:T(128)}, u32[]{:S(2)}) copy-start(s32[32]{0:T(128)} %param.15) | copy-start | bytes 388
  86.0 33.7 %copy-start.2 = (bf16[32,12,128]{2,0,1:T(8,128)(2,1)S(1)}, bf16[32,12,128]{2,0,1:T(8,128)(2,1)}, u32[]{:S(2)}) copy-start(bf16[32,12,128]{2,0,1:T(8,128)(2,1)} %param.12) | copy-start | bytes 294916
  114.2 17.1 %all-to-all-start.1 = ((bf16[8,16,1536]{2,1,0:T(8,128)(2,1)}), bf16[8,16,1536]{2,1,0:T(8,128)(2,1)S(1)}, u32[]{:S(2)}, u32[]{:S(2)}) async-start(bf16[8,16,1536]{2,1,0:T(8,128)(2,1)} %bitcast.34), calls=%async_computation.2 | async-start | bytes 786432 | tf_op jit(solution)/shard_map/all_to_all | solution.py:76
  120.9 3.5 %copy-start.3 = (f32[32,2]{0,1:T(2,128)S(1)}, f32[32,2]{0,1:T(2,128)}, u32[]{:S(2)}) copy-start(f32[32,2]{0,1:T(2,128)} %param.19) | copy-start | bytes 772
  120.9 10.4 %copy-start.1 = (bf16[32,1536]{1,0:T(8,128)(2,1)S(1)}, bf16[32,1536]{1,0:T(8,128)(2,1)}, u32[]{:S(2)}) copy-start(bf16[32,1536]{1,0:T(8,128)(2,1)} %param.16) | copy-start | bytes 294916
Sparse Core Ops, SparseCore 0:
  37.8 18.3 all-gather.1
  86.1 27.9 reduce-scatter.1
where the time goes:
time: 139 us
  waiting for transfers between devices  53.3 us (38%)
  matrix products  35.6 us (26%)
  blocking collectives  25 us (18%)
  between operations  14.1 us (10%)
  starting transfers between devices  5.59 us (4%)
  other arithmetic  3.26 us (2%)
  local copies, waits for them, and re-layouts  2.08 us (1%)
    reduce_scatter x1, waiting for transfers between devices, on_device(): lax.psum_scatter(down_terms.astype(jnp.bfloat16), 'mp', scatter_dimension...  28.1 us
    dot_general x1, matrix products, on_device(): down_terms = jnp.dot(hidden, w_down[0], preferred_element_type=jnp.float32)  19.4 us
    all_gather x1, waiting for transfers between devices, on_device(): piece = lax.all_gather(slot_rows, 'mp', axis=1, tiled=True)  18.4 us
    all_to_all x1, blocking collectives, on_device(): lax.all_to_all(outgoing, 'expert', split_axis=0, concat_axis=0, tiled=True)  16.6 us
    dot_general x1, matrix products, on_device(): gate_sum = jnp.dot(piece, gate_matrix, preferred_element_type=jnp.float32)  10.4 us
    psum x1, blocking collectives, on_device(): square_sum = lax.psum(jnp.sum(residual * residual, axis=1), 'mp')  8.37 us
    all_to_all x1, waiting for transfers between devices, on_device(): lax.all_to_all(result.astype(jnp.bfloat16), 'expert', split_axis=0, conca...  6.79 us
    all_to_all x1, starting transfers between devices, on_device(): lax.all_to_all(result.astype(jnp.bfloat16), 'expert', split_axis=0, conca...  5.51 us
  transfers between devices with their start and end apart: 3, of which 3 were waited for; matrix products, arithmetic and copies ran while one was open for 3% of the time, Pallas kernels for 0%

commit v1 on v0

--- a/solution.py
+++ b/solution.py
@@ -6,6 +6,12 @@
 D = 6144
 EXPERTS = 8
 TOP = 2
+
+
+def add_all(block, name):
+    shards = lax.all_gather(block, name, axis=0, tiled=False)
+    summed = shards.sum(axis=0)
+    return summed
 
 
 def on_device(
@@ -42,7 +48,7 @@
     split_count = experts_total // EXPERTS
     slot_count = tok_rows // 2
     residual = moe_input.astype(jnp.float32)
-    square_sum = lax.psum(jnp.sum(residual * residual, axis=1), "mp")
+    square_sum = add_all(jnp.sum(residual * residual, axis=1), "mp")
     normed = (residual * lax.rsqrt(square_sum / D + 1e-05)[:, None] * norm_gain[None, :]).astype(
         jnp.bfloat16
     )

time: 139 us -> 142 us (1.022)
  local copies, waits for them, and re-layouts: 2.08 us -> 3.65 us
    psum x1 -> x0, blocking collectives: 8.37 us -> none  [on_device(): square_sum = lax.psum(jnp.sum(residual * residual, axis=1), 'mp')]
    unnamed x0 -> x1, blocking collectives: none -> 8.34 us
    unnamed x11 -> x14, local copies, waits for them, and re-layouts: 0.93 us -> 2.41 us
where the time goes in v1:
time: 142 us; the launch traced here: 141 us
  waiting for transfers between devices  53.4 us (38%)
  matrix products  35.6 us (25%)
  blocking collectives  24.9 us (18%)
  between operations  14.8 us (10%)
  starting transfers between devices  5.6 us (4%)
  local copies, waits for them, and re-layouts  3.65 us (3%)
  other arithmetic  3.28 us (2%)
    reduce_scatter x1, waiting for transfers between devices, on_device(): lax.psum_scatter(down_terms.astype(jnp.bfloat16), 'mp', scatter_dimension...  28.1 us
    dot_general x1, matrix products, on_device(): down_terms = jnp.dot(hidden, w_down[0], preferred_element_type=jnp.float32)  19.4 us
    all_gather x1, waiting for transfers between devices, on_device(): piece = lax.all_gather(slot_rows, 'mp', axis=1, tiled=True)  18.5 us
    all_to_all x1, blocking collectives, on_device(): lax.all_to_all(outgoing, 'expert', split_axis=0, concat_axis=0, tiled=True)  16.6 us
    dot_general x1, matrix products, on_device(): gate_sum = jnp.dot(piece, gate_matrix, preferred_element_type=jnp.float32)  10.4 us
    unnamed x1, blocking collectives  8.34 us
    all_to_all x1, waiting for transfers between devices, on_device(): lax.all_to_all(result.astype(jnp.bfloat16), 'expert', split_axis=0, conca...  6.8 us
    all_to_all x1, starting transfers between devices, on_device(): lax.all_to_all(result.astype(jnp.bfloat16), 'expert', split_axis=0, conca...  5.52 us
  transfers between devices with their start and end apart: 3, of which 3 were waited for; matrix products, arithmetic and copies ran while one was open for 3% of the time, Pallas kernels for 0%

profile of v1, /device:TPU:0, one launch (start us, length us, event | category | flops | bytes accessed | tf_op | source)
XLA Modules:
  0.0 141.3 jit_solution(1134338209041496504)
XLA Ops:
  7.2 0.0 copy-start
  7.2 0.0 all-gather.3.cloned.1.call-start
  7.2 0.9 copy.35
  8.1 0.1 eq.31
  8.2 0.1 fusion.36
  8.3 0.1 reduce_window_sum.11
  8.4 0.8 select_reduce_fusion.1
  9.3 0.1 reduce_sum.73
  9.4 0.1 reduce_sum.75
  9.5 0.1 copy.36
  9.6 0.1 copy.37
  9.7 0.7 multiply_add_fusion
  10.4 1.0 fusion.28
  11.4 1.2 dynamic-slice
  13.3 0.2 dynamic-update-slice
  13.5 8.3 %all-reduce = f32[128]{0:T(128)S(1)} all-reduce(f32[128]{0:T(128)S(1)} %dynamic-update-slice), channel_id=2, replica_groups=mesh['expert'=8,'mp'=4] {'mp'}, use_global_device_ids=true, to_apply=%add | all-reduce | flops 128 | bytes 1024
  21.9 0.1 reshape.103
  22.0 0.1 convert_reduce_fusion
  22.1 1.2 convolution_convert_fusion
  23.3 16.6 %all_to_all.10 = bf16[8,16,1536]{2,1,0:T(8,128)(2,1)} all-to-all(bf16[8,16,1536]{2,1,0:T(8,128)(2,1)S(1)} %bitcast.34), channel_id=1, replica_groups=mesh['expert'=8,'mp'=4] {'expert'}, dimensions={0} | all-to-all | bytes 786432 | tf_op jit(solution)/shard_map/all_to_all | solution.py:69
  39.9 0.0 all-gather.3.cloned.1.call-update
  39.9 0.0 reduce-scatter.2.cloned.1.call-start
  39.9 18.5 %all-gather.3.cloned.1.call-done = bf16[128,6144]{1,0:T(8,128)(2,1)} async-done(((bf16[128,1536]{1,0:T(8,128)(2,1)}), bf16[128,6144]{1,0:T(8,128)(2,1)}) %all-gather.3.cloned.1.call-update) | async-done | bytes 1572880 | tf_op jit(solution)/shard_map/all_gather | solution.py:73
  58.4 10.4 %fusion.5 = f32[128,2048]{1,0:T(8,128)S(1)} fusion(bf16[128,6144]{1,0:T(8,128)(2,1)} %all-gather.3.cloned.1.call-done, bf16[1,6144,2048]{2,1,0:T(8,128)(2,1)} %param.21), kind=kOutput, calls=%fused_computation.5 | convolution fusion | flops 3221225472 | bytes 27787264 | tf_op jit(solution)/shard_map/dot_general | solution.py:74
  68.8 0.0 copy-start.4
  68.8 19.4 %fusion.7 = bf16[128,6144]{1,0:T(8,128)(2,1)} fusion(bf16[1,2048,6144]{2,1,0:T(8,128)(2,1)} %param.23, bf16[128,6144]{1,0:T(8,128)(2,1)} %all-gather.3.cloned.1.call-done, bf16[1,6144,2048]{2,1,0:T(8,128)(2,1)} %param.22, f32[128,2048]{1,0:T(8,128)S(1)} %fusion.5), kind=kOutput, calls=%fused_computation.7 | convolution fusion | flops 6444810240 | bytes 54525952 | tf_op jit(solution)/shard_map/dot_general | solution.py:77
  88.2 0.0 copy-start.2
  88.2 0.0 reduce-scatter.2.cloned.1.call-update
  88.2 0.0 copy-done.4
  88.3 0.1 iota_compare_fusion.2
  88.3 28.1 %reduce-scatter.2.cloned.1.call-done = bf16[128,1536]{1,0:T(8,128)(2,1)} async-done(((bf16[128,6144]{1,0:T(8,128)(2,1)}), bf16[128,1536]{1,0:T(8,128)(2,1)}) %reduce-scatter.2.cloned.1.call-update) | async-done | bytes 393232 | tf_op jit(solution)/shard_map/reduce_scatter | solution.py:78
  116.4 5.5 %all-to-all-start.1 = ((bf16[8,16,1536]{2,1,0:T(8,128)(2,1)}), bf16[8,16,1536]{2,1,0:T(8,128)(2,1)S(1)}, u32[]{:S(2)}, u32[]{:S(2)}) async-start(bf16[8,16,1536]{2,1,0:T(8,128)(2,1)} %bitcast.35), calls=%async_computation.2 | async-start | bytes 786432 | tf_op jit(solution)/shard_map/all_to_all | solution.py:82
  122.0 0.0 copy-done
  122.0 0.0 copy-done.2
  122.0 1.2 fusion.20
  123.2 0.0 copy-start.3
  123.2 0.0 copy-start.1
  123.2 0.3 fusion.40
  123.4 2.5 %convolution_convert_fusion.1 = bf16[32,2,6,128]{3,2,1,0:T(8,128)(2,1)S(1)} fusion(bf16[32,2,128,128]{3,2,1,0:T(8,128)(2,1)} %param.14, f32[32,2,6]{2,1,0:T(2,128)S(1)} %fusion.40, f32[32,2,6,128]{3,2,1,0:T(8,128)S(1)} %fusion.20), kind=kOutput, calls=%fused_computation.17 | convolution fusion | flops 12780031 | bytes 2393600 | tf_op jit(solution)/shard_map/bjgp,bjpd->bjgd/dot_general | solution.py:44
  126.0 0.7 copy.34
  126.6 0.0 copy-done.3
  126.6 0.1 select_reduce_fusion
  126.7 6.8 %all-to-all-done.1 = bf16[8,16,1536]{2,1,0:T(8,128)(2,1)S(1)} async-done(((bf16[8,16,1536]{2,1,0:T(8,128)(2,1)}), bf16[8,16,1536]{2,1,0:T(8,128)(2,1)S(1)}, u32[]{:S(2)}, u32[]{:S(2)}) %all-to-all-start.1) | async-done | bytes 393248 | tf_op jit(solution)/shard_map/all_to_all | solution.py:82
  133.5 0.0 copy-done.1
  133.5 0.9 fusion.18
  (4 shorter events, 0.0 us)
Async XLA Ops:
  7.2 114.8 %copy-start = (bf16[32,2,128,128]{3,2,1,0:T(8,128)(2,1)S(1)}, bf16[32,2,128,128]{3,2,1,0:T(8,128)(2,1)}, u32[]{:S(2)}) copy-start(bf16[32,2,128,128]{3,2,1,0:T(8,128)(2,1)} %param.13) | copy-start | bytes 6291460
  7.2 51.2 %all-gather.3.cloned.1.call-start = ((), (), s32[]{:S(2)}) async-start(), calls=%async_computation.3 | async-start | bytes 1966080 | tf_op jit(solution)/shard_map/all_gather | solution.py:73
  39.9 76.6 %reduce-scatter.2.cloned.1.call-start = ((), (), s32[]{:S(2)}) async-start(), calls=%async_computation.4 | async-start | bytes 1966080 | tf_op jit(solution)/shard_map/reduce_scatter | solution.py:78
  68.8 19.4 %copy-start.4 = (s32[32]{0:T(128)S(1)}, s32[32]{0:T(128)}, u32[]{:S(2)}) copy-start(s32[32]{0:T(128)} %param.15) | copy-start | bytes 388
  88.2 33.8 %copy-start.2 = (bf16[32,12,128]{2,0,1:T(8,128)(2,1)S(1)}, bf16[32,12,128]{2,0,1:T(8,128)(2,1)}, u32[]{:S(2)}) copy-start(bf16[32,12,128]{2,0,1:T(8,128)(2,1)} %param.12) | copy-start | bytes 294916
  116.4 17.1 %all-to-all-start.1 = ((bf16[8,16,1536]{2,1,0:T(8,128)(2,1)}), bf16[8,16,1536]{2,1,0:T(8,128)(2,1)S(1)}, u32[]{:S(2)}, u32[]{:S(2)}) async-start(bf16[8,16,1536]{2,1,0:T(8,128)(2,1)} %bitcast.35), calls=%async_computation.2 | async-start | bytes 786432 | tf_op jit(solution)/shard_map/all_to_all | solution.py:82
  123.2 3.5 %copy-start.3 = (f32[32,2]{0,1:T(2,128)S(1)}, f32[32,2]{0,1:T(2,128)}, u32[]{:S(2)}) copy-start(f32[32,2]{0,1:T(2,128)} %param.19) | copy-start | bytes 772
  123.2 10.4 %copy-start.1 = (bf16[32,1536]{1,0:T(8,128)(2,1)S(1)}, bf16[32,1536]{1,0:T(8,128)(2,1)}, u32[]{:S(2)}) copy-start(bf16[32,1536]{1,0:T(8,128)(2,1)} %param.16) | copy-start | bytes 294916
Sparse Core Ops, SparseCore 0:
  40.0 18.3 all-gather.2
  88.4 28.0 reduce-scatter.1
